TPU v7x, 128 devices: a whole 4x4x4 slice. The times are simulated.
128 devices in a mesh: pb: 128 (over z, x, y, core).
Axes of the slice: x: 4, y: 4, z: 4, core: 2. Of those that a mesh axis runs over, the one named last changes fastest.
Arguments:
- densities: bfloat16 [128, 128, 32, 1200], P(None, 'pb'), may hold values from -1.1953125 to 1.1953125
- screening: bfloat16 [128, 1200, 1200], P('pb'), may hold values from -0.1875 to 0.1875
- live: int32 [128, 128], P(None, 'pb'), may hold values 0 or 1
Outputs:
- kernel: bfloat16 [128, 128, 256], P(None, 'pb')
All inputs are finite; a program needn't handle non-finite values. No bound on the sum of `live` on one device may be relied on, other than what follows from the above.
Results may differ from a plain program's by a relative error of at most 0.0049.
Values may be sent and summed in bfloat16 or wider, within the bound.
A program may use at most 128 MiB of HBM per device.

v0:
```python
import jax
import jax.numpy as jnp
from jax import lax
from jax.sharding import PartitionSpec as P


def screen_rows(valence, weights):
    return jnp.einsum("nkbh,gh->nkbg", valence, weights, preferred_element_type=jnp.float32).astype(
        jnp.bfloat16
    )


def pair_blocks_of(conduction, screened):
    blocks = jnp.einsum("nkag,nkbg->nkab", conduction, screened, preferred_element_type=jnp.float32)
    return blocks.reshape(blocks.shape[0], blocks.shape[1], blocks.shape[2] * blocks.shape[3])


def on_device(densities, screening, live):
    pairs = densities.shape[2] // 2
    weights = screening[0]
    arrived = lax.all_to_all(densities, "pb", split_axis=0, concat_axis=0, tiled=True)
    screened = screen_rows(arrived[:, :, pairs:, :], weights)
    blocks = pair_blocks_of(arrived[:, :, :pairs, :], screened)
    result = lax.all_to_all(
        blocks.astype(jnp.bfloat16), "pb", split_axis=0, concat_axis=0, tiled=True
    )
    return result * live.astype(jnp.bfloat16)[:, :, None]


def solution(mesh):
    in_specs = (P(None, "pb", None, None), P("pb", None, None), P(None, "pb"))
    out_specs = P(None, "pb", None)
    return jax.shard_map(
        on_device, mesh=mesh, in_specs=in_specs, out_specs=out_specs, check_vma=False
    )
```

profile of v0, /device:TPU:1, one launch (start us, length us, event | category | flops | bytes accessed | tf_op | source)
XLA Modules:
  0.0 208.1 jit_solution(606226527447921767)
XLA Ops:
  0.0 0.0 copy-start
  0.0 16.6 %copy.8 = bf16[128,1,32,1200]{3,2,1,0:T(8,128)(2,1)} copy(bf16[128,1,32,1200]{0,3,2,1:T(8,128)(2,1)} %param.3) | data formatting | bytes 19660800 | tf_op args[0]
  16.6 131.9 %all_to_all.10 = bf16[128,1,32,1200]{3,2,1,0:T(8,128)(2,1)S(1)} all-to-all(bf16[128,1,32,1200]{3,2,1,0:T(8,128)(2,1)} %copy.8), channel_id=1, replica_groups=mesh['pb'=128] {'pb'}, dimensions={0} | all-to-all | bytes 19660800 | tf_op jit(solution)/shard_map/all_to_all | solution.py:21
  148.5 0.0 copy-start.1
  148.5 4.0 %copy-done.1 = bf16[128,1,32,1200]{3,2,1,0:T(8,128)(2,1)} copy-done((bf16[128,1,32,1200]{3,2,1,0:T(8,128)(2,1)}, bf16[128,1,32,1200]{3,2,1,0:T(8,128)(2,1)S(1)}, u32[]{:S(2)}) %copy-start.1) | copy-done | bytes 9830424
  152.5 2.8 %slice.8 = bf16[128,1,16,1200]{3,2,1,0:T(8,128)(2,1)} slice(bf16[128,1,32,1200]{3,2,1,0:T(8,128)(2,1)S(1)} %all_to_all.10), slice={[0:128], [0:1], [16:32], [0:1200]} | slice | bytes 9830400 | tf_op jit(solution)/shard_map/slice | solution.py:22
  155.3 8.5 %copy.15 = bf16[128,1,16,1200]{0,3,2,1:T(8,128)(2,1)} copy(bf16[128,1,16,1200]{3,2,1,0:T(8,128)(2,1)} %slice.8) | data formatting | bytes 9830400
  163.7 0.0 copy-done
  163.7 10.4 %convolution_convert_fusion = bf16[128,16,1200]{0,2,1:T(8,128)(2,1)} fusion(bf16[128,1,16,1200]{0,3,2,1:T(8,128)(2,1)} %copy.15, bf16[1,1200,1200]{2,1,0:T(8,128)(2,1)S(1)} %copy-done), kind=kOutput, calls=%fused_computation | convolution fusion | flops 5900697600 | bytes 12710400 | tf_op jit(solution)/shard_map/nkbh,gh->nkbg/dot_general | solution.py:8
  174.2 8.6 %copy.11 = bf16[128,16,1200]{2,1,0:T(8,128)(2,1)} copy(bf16[128,16,1200]{0,2,1:T(8,128)(2,1)} %convolution_convert_fusion) | data formatting | bytes 9830400 | tf_op jit(solution)/shard_map/convert_element_type | solution.py:8
  182.8 0.0 copy-start.2
  182.8 6.9 %fusion.4 = bf16[128,16,16]{1,2,0:T(8,128)(2,1)} fusion(bf16[128,16,1200]{2,1,0:T(8,128)(2,1)} %copy.11, bf16[128,1,32,1200]{3,2,0,1:T(8,128)(2,1)} %bitcast.21), kind=kOutput, calls=%fused_computation.6 | convolution fusion | flops 78675968 | bytes 10551296 | tf_op jit(solution)/shard_map/nkag,nkbg->nkab/dot_general | solution.py:14
  189.8 1.5 copy.12
  191.3 0.5 broadcast.1
  191.8 0.7 reduce
  192.4 0.1 copy.16
  192.6 0.7 reshape.32
  193.2 4.3 %all-to-all-start.1 = ((bf16[128,2,128]{2,1,0:T(2,128)(2,1)}), bf16[128,2,128]{2,1,0:T(2,128)(2,1)S(1)}, u32[]{:S(2)}, u32[]{:S(2)}) async-start(bf16[128,2,128]{2,1,0:T(2,128)(2,1)} %reshape.32), calls=%async_computation.1 | async-start | bytes 131072 | tf_op jit(solution)/shard_map/all_to_all | solution.py:24
  197.5 0.0 copy-done.2
  197.5 9.6 %all-to-all-done.1 = bf16[128,2,128]{2,1,0:T(2,128)(2,1)S(1)} async-done(((bf16[128,2,128]{2,1,0:T(2,128)(2,1)}), bf16[128,2,128]{2,1,0:T(2,128)(2,1)S(1)}, u32[]{:S(2)}, u32[]{:S(2)}) %all-to-all-start.1) | async-done | bytes 65568 | tf_op jit(solution)/shard_map/all_to_all | solution.py:24
  207.2 0.2 broadcast_multiply_fusion
  207.4 0.6 copy.14
  (2 shorter events, 0.0 us)
Async XLA Ops:
  0.0 163.7 %copy-start = (bf16[1,1200,1200]{2,1,0:T(8,128)(2,1)S(1)}, bf16[1,1200,1200]{2,1,0:T(8,128)(2,1)}, u32[]{:S(2)}) copy-start(bf16[1,1200,1200]{2,1,0:T(8,128)(2,1)} %param.4) | copy-start | bytes 8640004
  148.5 4.0 %copy-start.1 = (bf16[128,1,32,1200]{3,2,1,0:T(8,128)(2,1)}, bf16[128,1,32,1200]{3,2,1,0:T(8,128)(2,1)S(1)}, u32[]{:S(2)}) copy-start(bf16[128,1,32,1200]{3,2,1,0:T(8,128)(2,1)S(1)} %all_to_all.10) | copy-start | bytes 29491204
  182.8 14.7 %copy-start.2 = (s32[128,1]{0,1:T(1,128)S(1)}, s32[128,1]{0,1:T(1,128)}, u32[]{:S(2)}) copy-start(s32[128,1]{0,1:T(1,128)} %param.5) | copy-start | bytes 1540
  193.2 14.0 %all-to-all-start.1 = ((bf16[128,2,128]{2,1,0:T(2,128)(2,1)}), bf16[128,2,128]{2,1,0:T(2,128)(2,1)S(1)}, u32[]{:S(2)}, u32[]{:S(2)}) async-start(bf16[128,2,128]{2,1,0:T(2,128)(2,1)} %reshape.32), calls=%async_computation.1 | async-start | bytes 131072 | tf_op jit(solution)/shard_map/all_to_all | solution.py:24
where the time goes:
time: 209 us; the launch traced here: 208 us
  blocking collectives  132 us (63%)
  local copies, waits for them, and re-layouts  43.9 us (21%)
  matrix products  17.4 us (8%)
  waiting for transfers between devices  9.65 us (5%)
  starting transfers between devices  4.29 us (2%)
    all_to_all x1, blocking collectives, on_device(): lax.all_to_all(densities, 'pb', split_axis=0, concat_axis=0, tiled=True)  132 us
    unnamed x11, local copies, waits for them, and re-layouts  29.8 us
    dot_general x1, matrix products, screen_rows(): jnp.einsum('nkbh,gh->nkbg', valence, weights, preferred_element_type=jnp....  10.4 us
    all_to_all x1, waiting for transfers between devices, on_device(): lax.all_to_all(blocks.astype(jnp.bfloat16), 'pb', split_axis=0, concat_ax...  9.65 us
    convert_element_type x1, local copies, waits for them, and re-layouts, screen_rows(): jnp.einsum('nkbh,gh->nkbg', valence, weights, preferred_element_type=jnp....  8.65 us
    dot_general x1, matrix products, pair_blocks_of(): jnp.einsum('nkag,nkbg->nkab', conduction, screened, preferred_element_typ...  6.92 us
    all_to_all x1, starting transfers between devices, on_device(): lax.all_to_all(blocks.astype(jnp.bfloat16), 'pb', split_axis=0, concat_ax...  4.29 us
  transfers between devices with their start and end apart: 1, of which 1 were waited for; matrix products, arithmetic and copies ran while one was open for 0% of the time, Pallas kernels for 0%

commit v1 on v0

v1 whole, which is shorter than its diff:
```python
import jax
import jax.numpy as jnp
from jax import lax
from jax.experimental import pallas as pl
from jax.experimental.pallas import tpu as pltpu
from jax.sharding import PartitionSpec as P

F32 = jnp.float32
BF16 = jnp.bfloat16
MESH = pl.DeviceIdType.MESH

DEV = 128
PAIRS = 16
NG = 1200
MAIN = 1152
TAIL = NG - MAIN
HALF = 64
LANES_A = MAIN + 128
LANES_B = MAIN
STEP = 59
GROUP = 16
GROUPS = DEV // GROUP
PARTS_A = ((0, 384), (384, LANES_A))


def digits(i):
    return lax.div(i, 32), lax.rem(lax.div(i, 8), 4), lax.rem(lax.div(i, 2), 4), lax.rem(i, 2)


def undigits(z, x, y, c):
    return ((z * 4 + x) * 4 + y) * 2 + c


def target(me, slot):
    z, x, y, c = digits(me)
    dz, dx, dy, dc = digits(lax.rem(slot * STEP, DEV))
    return undigits(lax.rem(z + dz, 4), lax.rem(x + dx, 4), lax.rem(y + dy, 4), lax.rem(c + dc, 2))


def origin(me, slot):
    z, x, y, c = digits(me)
    dz, dx, dy, dc = digits(lax.rem(slot * STEP, DEV))
    return undigits(
        lax.rem(z + 4 - dz, 4), lax.rem(x + 4 - dx, 4), lax.rem(y + 4 - dy, 4), lax.rem(c + 2 - dc, 2)
    )


def same_block(shape, div0, mod0, div1, mod1):
    row = lax.broadcasted_iota(jnp.int32, shape, 0)
    col = lax.broadcasted_iota(jnp.int32, shape, 1)
    row = row // div0 if div0 > 1 else row % mod0
    col = col // div1 if div1 > 1 else col % mod1
    return row == col


def kernel(
    x_hbm, w_hbm, o_ref,
    xin, w_in, w_wide, send_a, send_b, recv_a, recv_b, screened, turn, spread, staged, landed,
    load_sem, send_sem, recv_sem_a, recv_sem_b, back_send_sem, back_recv_sem,
):
    me = lax.axis_index("pb")

    loads = [
        pltpu.make_async_copy(x_hbm.at[pl.ds(16, 16), pl.ds(0, 384)], xin.at[pl.ds(16, 16), pl.ds(0, 384)], load_sem.at[0]),
        pltpu.make_async_copy(x_hbm.at[pl.ds(16, 16), pl.ds(384, 816)], xin.at[pl.ds(16, 16), pl.ds(384, 816)], load_sem.at[1]),
        pltpu.make_async_copy(x_hbm.at[pl.ds(0, 16), pl.ds(MAIN, TAIL)], xin.at[pl.ds(0, 16), pl.ds(MAIN, TAIL)], load_sem.at[2]),
        pltpu.make_async_copy(x_hbm.at[pl.ds(0, 16), pl.ds(0, MAIN)], xin.at[pl.ds(0, 16), pl.ds(0, MAIN)], load_sem.at[3]),
        pltpu.make_async_copy(w_hbm, w_in, load_sem.at[4]),
    ]
    for load in loads:
        load.start()

    barrier = pltpu.get_barrier_semaphore()

    def greet(slot, _):
        pl.semaphore_signal(barrier, inc=1, device_id=(target(me, slot),), device_id_type=MESH)
        return 0

    lax.fori_loop(1, DEV, greet, 0)

    def turned(block):
        return jnp.transpose(block).astype(F32)

    def turn_block(first_row, column, slot, out, out_column):
        for r in range(PAIRS):
            turn[slot, :, r, :] = turned(xin[first_row + r, pl.ds(column, 128), :])
        out[:, :, pl.ds(out_column, 128)] = turn[slot].astype(BF16)

    def turn_blocks(first_row, begin, end, out):
        def body(j, _):
            column = pl.multiple_of(j * 128, 128)
            turn_block(first_row, column, lax.rem(j, 2), out, column)
            return 0

        lax.fori_loop(begin, end, body, 0)

    def send_part(src, dst, begin, width, sem_s, sem_r):
        def body(slot, _):
            to = target(me, slot)
            pltpu.make_async_remote_copy(
                src.at[to, :, pl.ds(begin, width)],
                dst.at[slot, :, pl.ds(begin, width)],
                sem_s,
                sem_r.at[lax.div(slot, GROUP)],
                device_id=(to,),
                device_id_type=MESH,
            ).start()
            return 0

        lax.fori_loop(1, DEV, body, 0)
        pltpu.make_async_copy(
            src.at[me, :, pl.ds(begin, width)], dst.at[0, :, pl.ds(begin, width)], sem_r.at[0]
        ).start()

    (a0, a1), (_, a2) = PARTS_A
    loads[0].wait()
    turn_blocks(16, 0, 3, send_a)
    pl.semaphore_wait(barrier, DEV - 1)
    send_part(send_a, recv_a, a0, a1 - a0, send_sem.at[0], recv_sem_a.at[0])
    loads[1].wait()
    loads[2].wait()
    turn_blocks(16, 3, 9, send_a)
    for r in range(PAIRS):
        gap = jnp.zeros((HALF - TAIL, 128), BF16)
        both = [xin[16 + r, MAIN:NG, :], gap, xin[r, MAIN:NG, :], gap]
        turn[1, :, r, :] = turned(jnp.concatenate(both, axis=0))
    send_a[:, :, MAIN:LANES_A] = turn[1].astype(BF16)
    send_part(send_a, recv_a, a1, a2 - a1, send_sem.at[1], recv_sem_a.at[1])
    loads[3].wait()
    turn_blocks(0, 0, 9, send_b)
    send_part(send_b, recv_b, 0, LANES_B, send_sem.at[2], recv_sem_b)

    loads[4].wait()
    w_wide[...] = jnp.zeros_like(w_wide)
    w_wide[pl.ds(HALF, TAIL), pl.ds(0, NG)] = w_in[pl.ds(MAIN, TAIL), :]
    w_wide[pl.ds(128, MAIN), pl.ds(0, NG)] = w_in[pl.ds(0, MAIN), :]
    spread[...] = same_block((256, 256), 1, 16, 1, 16).astype(BF16)

    def screen(g, _):
        slots = pl.ds(g * GROUP, GROUP)
        for p, (begin, end) in enumerate(PARTS_A):
            view = recv_a.at[slots, :, pl.ds(begin, end - begin)]
            pltpu.make_async_copy(view, view, recv_sem_a.at[p, g]).wait()
        left = recv_a[slots].reshape(GROUP * PAIRS, LANES_A)

        def column(n, _):
            rows = pl.ds(pl.multiple_of(n * 256, 256), 256)
            part = lax.dot_general(left, w_wide[rows, :], (((1,), (1,)), ((), ())), preferred_element_type=F32)
            screened[g, :, rows] = part.astype(BF16)
            return 0

        lax.fori_loop(0, 5, column, 0)
        return 0

    lax.fori_loop(0, GROUPS, screen, 0)

    def contract(g, _):
        slots = pl.ds(g * GROUP, GROUP)
        view = recv_b.at[slots]
        pltpu.make_async_copy(view, view, recv_sem_b.at[g]).wait()
        tails = recv_a[slots, :, MAIN:LANES_A].reshape(GROUP * PAIRS, 128)
        mains = recv_b[slots].reshape(GROUP * PAIRS, MAIN)
        nt = (((1,), (1,)), ((), ()))
        every = lax.dot_general(mains, screened[g, :, 128:], nt, preferred_element_type=F32)
        every = every + lax.dot_general(tails, screened[g, :, :128], nt, preferred_element_type=F32)
        own = jnp.where(same_block((256, 256), 16, 0, 16, 0), every, 0.0).astype(BF16)
        wide = jnp.dot(own, spread[...], preferred_element_type=F32)
        wide = jnp.where(same_block((256, 256), 1, 16, 16, 0), wide, 0.0).astype(BF16)
        gather = same_block((GROUP, 256), 1, GROUP, 16, 0).astype(BF16)
        rows = jnp.dot(gather, wide, preferred_element_type=F32)
        staged[slots, 0, :] = rows[:, :128]
        staged[slots, 1, :] = rows[:, 128:]

        def give_back(i, _):
            slot = g * GROUP + i
            to = origin(me, slot)
            pltpu.make_async_remote_copy(
                staged.at[slot], landed.at[me], back_send_sem, back_recv_sem,
                device_id=(to,), device_id_type=MESH,
            ).start()
            return 0

        lax.fori_loop(jnp.where(g == 0, 1, 0), GROUP, give_back, 0)
        return 0

    lax.fori_loop(0, GROUPS, contract, 0)
    pltpu.make_async_copy(staged.at[0], landed.at[me], back_recv_sem).start()

    for p, (begin, end) in enumerate(PARTS_A):
        view = send_a.at[pl.ds(1, DEV - 1), :, pl.ds(begin, end - begin)]
        pltpu.make_async_copy(view, view, send_sem.at[p]).wait()
    view = send_b.at[pl.ds(1, DEV - 1)]
    pltpu.make_async_copy(view, view, send_sem.at[2]).wait()
    view = staged.at[pl.ds(1, DEV - 1)]
    pltpu.make_async_copy(view, view, back_send_sem).wait()
    pltpu.make_async_copy(landed, landed, back_recv_sem).wait()
    o_ref[:, :128] = landed[:, 0, :]
    o_ref[:, 128:] = landed[:, 1, :]


def on_device(densities, screening, live):
    x = jnp.transpose(densities, (1, 2, 3, 0))[0]
    blocks = pl.pallas_call(
        kernel,
        out_shape=jax.ShapeDtypeStruct((DEV, PAIRS * PAIRS), F32),
        in_specs=[pl.BlockSpec(memory_space=pl.ANY)] * 2,
        out_specs=pl.BlockSpec(memory_space=pltpu.VMEM),
        scratch_shapes=[
            pltpu.VMEM((2 * PAIRS, NG, DEV), BF16),
            pltpu.VMEM((NG, NG), BF16),
            pltpu.VMEM((LANES_A, LANES_A), BF16),
            pltpu.VMEM((DEV, PAIRS, LANES_A), BF16),
            pltpu.VMEM((DEV, PAIRS, LANES_B), BF16),
            pltpu.VMEM((DEV, PAIRS, LANES_A), BF16),
            pltpu.VMEM((DEV, PAIRS, LANES_B), BF16),
            pltpu.VMEM((GROUPS, GROUP * PAIRS, LANES_A), BF16),
            pltpu.VMEM((2, DEV, PAIRS, 128), F32),
            pltpu.VMEM((256, 256), BF16),
            pltpu.VMEM((DEV, 2, 128), F32),
            pltpu.VMEM((DEV, 2, 128), F32),
            pltpu.SemaphoreType.DMA((5,)),
            pltpu.SemaphoreType.DMA((3,)),
            pltpu.SemaphoreType.DMA((2, GROUPS)),
            pltpu.SemaphoreType.DMA((GROUPS,)),
            pltpu.SemaphoreType.DMA,
            pltpu.SemaphoreType.DMA,
        ],
        compiler_params=pltpu.CompilerParams(
            collective_id=0, has_side_effects=True, vmem_limit_bytes=58 << 20
        ),
    )(x, screening[0])
    return (blocks * live.astype(F32)).astype(BF16)[:, None, :]


def solution(mesh):
    in_specs = (P(None, "pb", None, None), P("pb", None, None), P(None, "pb"))
    return jax.shard_map(
        on_device, mesh=mesh, in_specs=in_specs, out_specs=P(None, "pb", None), check_vma=False
    )
```

time: 209 us -> 138 us (0.66)
  Pallas kernels: 0 us -> 135 us
  blocking collectives: 132 us -> 0 us
  local copies, waits for them, and re-layouts: 43.9 us -> 0 us
  matrix products: 17.4 us -> 0 us
  waiting for transfers between devices: 9.65 us -> 0 us
  starting transfers between devices: 4.29 us -> 0 us
    pallas_call x0 -> x1, Pallas kernels: none -> 135 us  [on_device(): pl.pallas_call(kernel, out_shape=jax.ShapeDtypeStruct((DEV, PAIRS * PAIRS...]
    all_to_all x1 -> x0, blocking collectives: 132 us -> none  [on_device(): lax.all_to_all(densities, 'pb', split_axis=0, concat_axis=0, tiled=True)]
    unnamed x11 -> x0, local copies, waits for them, and re-layouts: 29.8 us -> none
    dot_general x2 -> x0, matrix products: 17.4 us -> none  [the longest x1 10.4 us: screen_rows(): jnp.einsum('nkbh,gh->nkbg', valence, weights, preferred_element_type=jnp....]
    convert_element_type x3 -> x0, local copies, waits for them, and re-layouts: 10.7 us -> none  [the longest x1 8.65 us: screen_rows(): jnp.einsum('nkbh,gh->nkbg', valence, weights, preferred_element_type=jnp....]
    all_to_all x1 -> x0, waiting for transfers between devices: 9.65 us -> none  [on_device(): lax.all_to_all(blocks.astype(jnp.bfloat16), 'pb', split_axis=0, concat_ax...]
    all_to_all x1 -> x0, starting transfers between devices: 4.29 us -> none  [on_device(): lax.all_to_all(blocks.astype(jnp.bfloat16), 'pb', split_axis=0, concat_ax...]
    slice x1 -> x0, local copies, waits for them, and re-layouts: 2.79 us -> none  [on_device(): screened = screen_rows(arrived[:, :, pairs:, :], weights)]
  transfers between devices with their start and end apart: 1 -> 0, of which waited for: 1 -> 0; matrix products, arithmetic and copies ran while one was open for 0% -> 0% of each run, Pallas kernels for 0% -> 0%
where the time goes in v1:
time: 138 us
  Pallas kernels  135 us (98%)
  other arithmetic  2.28 us (2%)
    pallas_call x1, Pallas kernels, on_device(): pl.pallas_call(kernel, out_shape=jax.ShapeDtypeStruct((DEV, PAIRS * PAIRS...  135 us

profile of v1, /device:TPU:1, one launch (start us, length us, event | category | flops | bytes accessed | tf_op | source)
XLA Modules:
  0.0 137.6 jit_solution(12399942465636418682)
XLA Ops:
  0.0 0.7 convert_bitcast_fusion
  0.7 135.3 %shard_map.37 = f32[128,256]{1,0:T(8,128)} custom-call(bf16[32,1200,128]{2,1,0:T(8,128)(2,1)} %bitcast.8, bf16[1200,1200]{1,0:T(8,128)(2,1)} %bitcast.9), custom_call_target="tpu_custom_call" | custom-call | tf_op jit(solution)/shard_map/pallas_call | solution.py:203
  136.0 1.6 %fusion = bf16[128,1,256]{2,0,1:T(8,128)(2,1)} fusion(f32[128,256]{1,0:T(8,128)} %shard_map.37, f32[128]{0:T(128)S(1)} %convert_bitcast_fusion), kind=kLoop, calls=%fused_computation.1 | loop fusion | flops 65536 | bytes 197120 | tf_op jit(solution)/shard_map/broadcast_in_dim | solution.py:232

commit v2 on v1

v2 whole, which is shorter than its diff:
```python
import jax
import jax.numpy as jnp
from jax import lax
from jax.experimental import pallas as pl
from jax.experimental.pallas import tpu as pltpu
from jax.sharding import PartitionSpec as P

F32 = jnp.float32
BF16 = jnp.bfloat16
MESH = pl.DeviceIdType.MESH

DEV = 128
PAIRS = 16
NG = 1200
MAIN = 1152
TAIL = NG - MAIN
HALF = 64
LANES_A = MAIN + 128
LANES_B = MAIN
STEP = 37
GROUP = 16
GROUPS = DEV // GROUP
FEW = 8
FEWS = DEV // FEW
ROWS = FEW * PAIRS
PARTS_A = ((0, 384), (384, LANES_A))


def digits(i):
    return i // 32, i // 8 % 4, i // 2 % 4, i % 2


def hops(i):
    return sum(min(d, 4 - d) for d in digits(i)[:3])


_MIXED = [i * STEP % DEV for i in range(1, DEV)]
ORDER = [0] + sorted(_MIXED, key=lambda i: hops(i) <= 1)


def fill_places(me, to_ref, from_ref):
    z, x, y, c = lax.div(me, 32), lax.rem(lax.div(me, 8), 4), lax.rem(lax.div(me, 2), 4), lax.rem(me, 2)
    at = [
        [lax.rem(own + d, size) * unit for d in range(size)]
        for own, size, unit in ((z, 4, 32), (x, 4, 8), (y, 4, 2), (c, 2, 1))
    ]
    for slot, offset in enumerate(ORDER):
        there = digits(offset)
        back = [-d % size for d, size in zip(there, (4, 4, 4, 2))]
        to_ref[slot] = sum(column[d] for column, d in zip(at, there))
        from_ref[slot] = sum(column[d] for column, d in zip(at, back))


def same_block(shape, div0, mod0, div1, mod1):
    row = lax.broadcasted_iota(jnp.int32, shape, 0)
    col = lax.broadcasted_iota(jnp.int32, shape, 1)
    row = row // div0 if div0 > 1 else row % mod0
    col = col // div1 if div1 > 1 else col % mod1
    return row == col


def kernel(
    x_hbm, w_hbm, live_ref, o_ref,
    xin, w_in, w_wide, send_a, send_b, recv_a, recv_b, screened, turn, spread, staged, landed,
    to_ref, from_ref, load_sem, send_sem, recv_sem_a, recv_sem_b, back_send_sem, back_recv_sem,
):
    me = lax.axis_index("pb")

    loads = [
        pltpu.make_async_copy(x_hbm.at[pl.ds(16, 16), pl.ds(0, 384)], xin.at[pl.ds(16, 16), pl.ds(0, 384)], load_sem.at[0]),
        pltpu.make_async_copy(x_hbm.at[pl.ds(16, 16), pl.ds(384, 816)], xin.at[pl.ds(16, 16), pl.ds(384, 816)], load_sem.at[1]),
        pltpu.make_async_copy(x_hbm.at[pl.ds(0, 16), pl.ds(MAIN, TAIL)], xin.at[pl.ds(0, 16), pl.ds(MAIN, TAIL)], load_sem.at[2]),
        pltpu.make_async_copy(x_hbm.at[pl.ds(0, 16), pl.ds(0, MAIN)], xin.at[pl.ds(0, 16), pl.ds(0, MAIN)], load_sem.at[3]),
        pltpu.make_async_copy(w_hbm, w_in, load_sem.at[4]),
    ]
    for load in loads:
        load.start()

    barrier = pltpu.get_barrier_semaphore()

    def greet(slot, _):
        pl.semaphore_signal(barrier, inc=1, device_id=(lax.rem(me + slot, DEV),), device_id_type=MESH)
        return 0

    lax.fori_loop(1, DEV, greet, 0)

    fill_places(me, to_ref, from_ref)

    def turned(block):
        return jnp.transpose(block).astype(F32)

    def turn_block(first_row, column, slot, out, out_column):
        for r in range(PAIRS):
            turn[slot, :, r, :] = turned(xin[first_row + r, pl.ds(column, 128), :])
        out[:, :, pl.ds(out_column, 128)] = turn[slot].astype(BF16)

    def turn_blocks(first_row, begin, end, out):
        def body(j, _):
            column = pl.multiple_of(j * 128, 128)
            turn_block(first_row, column, lax.rem(j, 2), out, column)
            return 0

        lax.fori_loop(begin, end, body, 0)

    def send_part(src, dst, begin, width, sem_s, sem_r, group):
        def body(slot, _):
            to = to_ref[slot]
            pltpu.make_async_remote_copy(
                src.at[to, :, pl.ds(begin, width)],
                dst.at[slot, :, pl.ds(begin, width)],
                sem_s,
                sem_r.at[lax.div(slot, group)],
                device_id=(to,),
                device_id_type=MESH,
            ).start()
            return 0

        lax.fori_loop(1, DEV, body, 0)
        pltpu.make_async_copy(
            src.at[me, :, pl.ds(begin, width)], dst.at[0, :, pl.ds(begin, width)], sem_r.at[0]
        ).start()

    (a0, a1), (_, a2) = PARTS_A
    loads[0].wait()
    turn_blocks(16, 0, 3, send_a)
    pl.semaphore_wait(barrier, DEV - 1)
    send_part(send_a, recv_a, a0, a1 - a0, send_sem.at[0], recv_sem_a.at[0], GROUP)
    loads[1].wait()
    loads[2].wait()
    turn_blocks(16, 3, 9, send_a)
    for r in range(PAIRS):
        gap = jnp.zeros((HALF - TAIL, 128), BF16)
        both = [xin[16 + r, MAIN:NG, :], gap, xin[r, MAIN:NG, :], gap]
        turn[1, :, r, :] = turned(jnp.concatenate(both, axis=0))
    send_a[:, :, MAIN:LANES_A] = turn[1].astype(BF16)
    send_part(send_a, recv_a, a1, a2 - a1, send_sem.at[1], recv_sem_a.at[1], GROUP)
    loads[3].wait()
    turn_blocks(0, 0, 9, send_b)
    send_part(send_b, recv_b, 0, LANES_B, send_sem.at[2], recv_sem_b, FEW)

    loads[4].wait()
    w_wide[...] = jnp.zeros_like(w_wide)
    w_wide[pl.ds(HALF, TAIL), pl.ds(0, NG)] = w_in[pl.ds(MAIN, TAIL), :]
    w_wide[pl.ds(128, MAIN), pl.ds(0, NG)] = w_in[pl.ds(0, MAIN), :]
    spread[...] = same_block((ROWS, 256), 1, 16, 1, 16).astype(BF16)

    def screen(g, _):
        slots = pl.ds(g * GROUP, GROUP)
        for p, (begin, end) in enumerate(PARTS_A):
            view = recv_a.at[slots, :, pl.ds(begin, end - begin)]
            pltpu.make_async_copy(view, view, recv_sem_a.at[p, g]).wait()
        left = recv_a[slots].reshape(GROUP * PAIRS, LANES_A)

        def column(n, _):
            rows = pl.ds(pl.multiple_of(n * 256, 256), 256)
            part = lax.dot_general(left, w_wide[rows, :], (((1,), (1,)), ((), ())), preferred_element_type=F32)
            screened[pl.ds(g * GROUP * PAIRS, GROUP * PAIRS), rows] = part.astype(BF16)
            return 0

        lax.fori_loop(0, 5, column, 0)
        return 0

    lax.fori_loop(0, GROUPS, screen, 0)

    def contract(g, _):
        slots = pl.ds(g * FEW, FEW)
        view = recv_b.at[slots]
        pltpu.make_async_copy(view, view, recv_sem_b.at[g]).wait()
        tails = recv_a[slots, :, MAIN:LANES_A].reshape(ROWS, 128)
        mains = recv_b[slots].reshape(ROWS, MAIN)
        right = screened[pl.ds(g * ROWS, ROWS), :]
        nt = (((1,), (1,)), ((), ()))
        every = lax.dot_general(mains, right[:, 128:], nt, preferred_element_type=F32)
        every = every + lax.dot_general(tails, right[:, :128], nt, preferred_element_type=F32)
        own = jnp.where(same_block((ROWS, ROWS), 16, 0, 16, 0), every, 0.0).astype(BF16)
        wide = jnp.dot(own, spread[...], preferred_element_type=F32)
        wide = jnp.where(same_block((ROWS, 256), 1, 16, 16, 0), wide, 0.0).astype(BF16)
        gather = same_block((FEW, ROWS), 1, FEW, 16, 0).astype(BF16)
        rows = jnp.dot(gather, wide, preferred_element_type=F32)
        staged[slots, 0, :] = rows[:, :128]
        staged[slots, 1, :] = rows[:, 128:]

        def give_back(i, _):
            slot = g * FEW + i
            pltpu.make_async_remote_copy(
                staged.at[slot], landed.at[me], back_send_sem, back_recv_sem,
                device_id=(from_ref[slot],), device_id_type=MESH,
            ).start()
            return 0

        lax.fori_loop(jnp.where(g == 0, 1, 0), FEW, give_back, 0)
        return 0

    kept = jnp.where(same_block((DEV, DEV), 1, DEV, 1, DEV), live_ref[...].astype(F32), 0.0).astype(BF16)

    def keep(rows):
        return jnp.dot(kept, rows.astype(BF16), preferred_element_type=F32).astype(BF16)

    lax.fori_loop(0, FEWS, contract, 0)
    pltpu.make_async_copy(staged.at[0], landed.at[me], back_recv_sem).start()

    for p, (begin, end) in enumerate(PARTS_A):
        view = send_a.at[pl.ds(1, DEV - 1), :, pl.ds(begin, end - begin)]
        pltpu.make_async_copy(view, view, send_sem.at[p]).wait()
    view = send_b.at[pl.ds(1, DEV - 1)]
    pltpu.make_async_copy(view, view, send_sem.at[2]).wait()
    view = staged.at[pl.ds(1, DEV - 1)]
    pltpu.make_async_copy(view, view, back_send_sem).wait()
    pltpu.make_async_copy(landed, landed, back_recv_sem).wait()
    o_ref[:, :128] = keep(landed[:, 0, :])
    o_ref[:, 128:] = keep(landed[:, 1, :])


def on_device(densities, screening, live):
    x = jnp.transpose(densities, (1, 2, 3, 0))[0]
    blocks = pl.pallas_call(
        kernel,
        out_shape=jax.ShapeDtypeStruct((DEV, PAIRS * PAIRS), BF16),
        in_specs=[pl.BlockSpec(memory_space=pl.ANY)] * 2 + [pl.BlockSpec(memory_space=pltpu.VMEM)],
        out_specs=pl.BlockSpec(memory_space=pltpu.VMEM),
        scratch_shapes=[
            pltpu.VMEM((2 * PAIRS, NG, DEV), BF16),
            pltpu.VMEM((NG, NG), BF16),
            pltpu.VMEM((LANES_A, LANES_A), BF16),
            pltpu.VMEM((DEV, PAIRS, LANES_A), BF16),
            pltpu.VMEM((DEV, PAIRS, LANES_B), BF16),
            pltpu.VMEM((DEV, PAIRS, LANES_A), BF16),
            pltpu.VMEM((DEV, PAIRS, LANES_B), BF16),
            pltpu.VMEM((DEV * PAIRS, LANES_A), BF16),
            pltpu.VMEM((2, DEV, PAIRS, 128), F32),
            pltpu.VMEM((ROWS, 256), BF16),
            pltpu.VMEM((DEV, 2, 128), F32),
            pltpu.VMEM((DEV, 2, 128), F32),
            pltpu.SMEM((DEV,), jnp.int32),
            pltpu.SMEM((DEV,), jnp.int32),
            pltpu.SemaphoreType.DMA((5,)),
            pltpu.SemaphoreType.DMA((3,)),
            pltpu.SemaphoreType.DMA((2, GROUPS)),
            pltpu.SemaphoreType.DMA((FEWS,)),
            pltpu.SemaphoreType.DMA,
            pltpu.SemaphoreType.DMA,
        ],
        compiler_params=pltpu.CompilerParams(
            collective_id=0, has_side_effects=True, vmem_limit_bytes=58 << 20
        ),
    )(x, screening[0], live.reshape(1, DEV))
    return blocks[:, None, :]


def solution(mesh):
    in_specs = (P(None, "pb", None, None), P("pb", None, None), P(None, "pb"))
    return jax.shard_map(
        on_device, mesh=mesh, in_specs=in_specs, out_specs=P(None, "pb", None), check_vma=False
    )
```

time: 138 us -> 129 us (0.935)
  Pallas kernels: 135 us -> 127 us
  other arithmetic: 2.28 us -> 0 us
  local copies, waits for them, and re-layouts: 0 us -> 1.47 us
    pallas_call x1, Pallas kernels: 135 us -> 127 us  [on_device(): pl.pallas_call(kernel, out_shape=jax.ShapeDtypeStruct((DEV, PAIRS * PAIRS...]
    broadcast_in_dim x1 -> x0, other arithmetic: 1.62 us -> none  [on_device(): return (blocks * live.astype(F32)).astype(BF16)[:, None, :]]
    unnamed x0 -> x1, local copies, waits for them, and re-layouts: none -> 1.47 us
where the time goes in v2:
time: 129 us; the launch traced here: 128 us
  Pallas kernels  127 us (98%)
  local copies, waits for them, and re-layouts  1.47 us (1%)
    pallas_call x1, Pallas kernels, on_device(): pl.pallas_call(kernel, out_shape=jax.ShapeDtypeStruct((DEV, PAIRS * PAIRS...  127 us

profile of v2, /device:TPU:1, one launch (start us, length us, event | category | flops | bytes accessed | tf_op | source)
XLA Modules:
  0.0 128.4 jit_solution(13347314722684570930)
XLA Ops:
  0.0 126.9 %shard_map.37 = bf16[128,256]{1,0:T(8,128)(2,1)} custom-call(bf16[32,1200,128]{2,1,0:T(8,128)(2,1)} %bitcast.6, bf16[1200,1200]{1,0:T(8,128)(2,1)} %bitcast.7, s32[1,128]{1,0:T(1,128)} %bitcast.9), custom_call_target="tpu_custom_call" | custom-call | tf_op jit(solution)/shard_map/pallas_call | solution.py:216
  127.0 1.5 %copy.5 = bf16[128,1,256]{2,0,1:T(8,128)(2,1)} copy(bf16[128,1,256]{2,0,1:T(8,128)(2,1)} %bitcast.8) | data formatting | bytes 131072

commit v3 on v2

--- a/solution.py
+++ b/solution.py
@@ -61,7 +61,7 @@
 
 def kernel(
     x_hbm, w_hbm, live_ref, o_ref,
-    xin, w_in, w_wide, send_a, send_b, recv_a, recv_b, screened, turn, spread, staged, landed,
+    xin, w_in, w_wide, send_a, send_b, recv_a, recv_b, screened, turn, spread, kept, staged, landed,
     to_ref, from_ref, load_sem, send_sem, recv_sem_a, recv_sem_b, back_send_sem, back_recv_sem,
 ):
     me = lax.axis_index("pb")
@@ -164,14 +164,14 @@
 
     def contract(g, _):
         slots = pl.ds(g * FEW, FEW)
+        nt = (((1,), (1,)), ((), ()))
+        tails = recv_a[slots, :, MAIN:LANES_A].reshape(ROWS, 128)
+        right = screened[pl.ds(g * ROWS, ROWS), :]
+        early = lax.dot_general(tails, right[:, :128], nt, preferred_element_type=F32)
         view = recv_b.at[slots]
         pltpu.make_async_copy(view, view, recv_sem_b.at[g]).wait()
-        tails = recv_a[slots, :, MAIN:LANES_A].reshape(ROWS, 128)
         mains = recv_b[slots].reshape(ROWS, MAIN)
-        right = screened[pl.ds(g * ROWS, ROWS), :]
-        nt = (((1,), (1,)), ((), ()))
-        every = lax.dot_general(mains, right[:, 128:], nt, preferred_element_type=F32)
-        every = every + lax.dot_general(tails, right[:, :128], nt, preferred_element_type=F32)
+        every = early + lax.dot_general(mains, right[:, 128:], nt, preferred_element_type=F32)
         own = jnp.where(same_block((ROWS, ROWS), 16, 0, 16, 0), every, 0.0).astype(BF16)
         wide = jnp.dot(own, spread[...], preferred_element_type=F32)
         wide = jnp.where(same_block((ROWS, 256), 1, 16, 16, 0), wide, 0.0).astype(BF16)
@@ -188,13 +188,17 @@
             ).start()
             return 0
 
-        lax.fori_loop(jnp.where(g == 0, 1, 0), FEW, give_back, 0)
+        @pl.when(g > 0)
+        def _():
+            give_back(0, 0)
+
+        for i in range(1, FEW):
+            give_back(i, 0)
         return 0
 
-    kept = jnp.where(same_block((DEV, DEV), 1, DEV, 1, DEV), live_ref[...].astype(F32), 0.0).astype(BF16)
-
-    def keep(rows):
-        return jnp.dot(kept, rows.astype(BF16), preferred_element_type=F32).astype(BF16)
+    ones = jnp.ones((DEV, 128), BF16)
+    diagonal = jnp.where(same_block((DEV, DEV), 1, DEV, 1, DEV), live_ref[...].astype(F32), 0.0).astype(BF16)
+    kept[...] = jnp.dot(diagonal, ones, preferred_element_type=F32)
 
     lax.fori_loop(0, FEWS, contract, 0)
     pltpu.make_async_copy(staged.at[0], landed.at[me], back_recv_sem).start()
@@ -207,8 +211,8 @@
     view = staged.at[pl.ds(1, DEV - 1)]
     pltpu.make_async_copy(view, view, back_send_sem).wait()
     pltpu.make_async_copy(landed, landed, back_recv_sem).wait()
-    o_ref[:, :128] = keep(landed[:, 0, :])
-    o_ref[:, 128:] = keep(landed[:, 1, :])
+    o_ref[:, :128] = (landed[:, 0, :] * kept[...]).astype(BF16)
+    o_ref[:, 128:] = (landed[:, 1, :] * kept[...]).astype(BF16)
 
 
 def on_device(densities, screening, live):
@@ -216,7 +220,7 @@
     blocks = pl.pallas_call(
         kernel,
         out_shape=jax.ShapeDtypeStruct((DEV, PAIRS * PAIRS), BF16),
-        in_specs=[pl.BlockSpec(memory_space=pl.ANY)] * 2 + [pl.BlockSpec(memory_space=pltpu.VMEM)],
+        in_specs=[pl.BlockSpec(memory_space=pltpu.HBM)] * 2 + [pl.BlockSpec(memory_space=pltpu.VMEM)],
         out_specs=pl.BlockSpec(memory_space=pltpu.VMEM),
         scratch_shapes=[
             pltpu.VMEM((2 * PAIRS, NG, DEV), BF16),
@@ -229,6 +233,7 @@
             pltpu.VMEM((DEV * PAIRS, LANES_A), BF16),
             pltpu.VMEM((2, DEV, PAIRS, 128), F32),
             pltpu.VMEM((ROWS, 256), BF16),
+            pltpu.VMEM((DEV, 128), F32),
             pltpu.VMEM((DEV, 2, 128), F32),
             pltpu.VMEM((DEV, 2, 128), F32),
             pltpu.SMEM((DEV,), jnp.int32),
@@ -241,7 +246,7 @@
             pltpu.SemaphoreType.DMA,
         ],
         compiler_params=pltpu.CompilerParams(
-            collective_id=0, has_side_effects=True, vmem_limit_bytes=58 << 20
+            collective_id=0, has_side_effects=True, vmem_limit_bytes=52 << 20
         ),
     )(x, screening[0], live.reshape(1, DEV))
     return blocks[:, None, :]

time: 129 us -> 127 us (0.984)
    pallas_call x1, Pallas kernels: 127 us -> 126 us  [on_device(): pl.pallas_call(kernel, out_shape=jax.ShapeDtypeStruct((DEV, PAIRS * PAIRS...]
where the time goes in v3:
time: 127 us
  Pallas kernels  126 us (99%)
  local copies, waits for them, and re-layouts  1.29 us (1%)
    pallas_call x1, Pallas kernels, on_device(): pl.pallas_call(kernel, out_shape=jax.ShapeDtypeStruct((DEV, PAIRS * PAIRS...  126 us

profile of v3, /device:TPU:1, one launch (start us, length us, event | category | flops | bytes accessed | tf_op | source)
XLA Modules:
  0.0 126.9 jit_solution(16417737005117281682)
XLA Ops:
  0.0 0.0 copy-start
  0.0 0.7 copy-done
  0.7 125.6 %shard_map.37 = bf16[128,256]{1,0:T(8,128)(2,1)S(1)} custom-call(bf16[32,1200,128]{2,1,0:T(8,128)(2,1)} %bitcast.8, bf16[1200,1200]{1,0:T(8,128)(2,1)} %bitcast.9, s32[1,128]{1,0:T(1,128)S(1)} %bitcast.7), custom_call_target="tpu_custom_call" | custom-call | tf_op jit(solution)/shard_map/pallas_call | solution.py:220
  126.2 0.6 copy.5
Async XLA Ops:
  0.0 0.7 copy-start

commit v4 on v3

--- a/solution.py
+++ b/solution.py
@@ -14,8 +14,9 @@
 NG = 1200
 MAIN = 1152
 TAIL = NG - MAIN
-HALF = 64
 LANES_A = MAIN + 128
+FULL = 12
+THIRD = 128 - 2 * TAIL
 LANES_B = MAIN
 STEP = 37
 GROUP = 16
@@ -23,7 +24,8 @@
 FEW = 8
 FEWS = DEV // FEW
 ROWS = FEW * PAIRS
-PARTS_A = ((0, 384), (384, LANES_A))
+FIRST = 384
+REST = MAIN - FIRST
 
 
 def digits(i):
@@ -60,29 +62,32 @@
 
 
 def kernel(
-    x_hbm, w_hbm, live_ref, o_ref,
-    xin, w_in, w_wide, send_a, send_b, recv_a, recv_b, screened, turn, spread, kept, staged, landed,
+    x_hbm, w_hbm, live_hbm, o_ref,
+    xin, w_in, w_wide, send_a, send_m, send_t, send_b, recv_a, recv_m, recv_t, recv_b, tails, lift, shift, screened, turn, spread, live_ref, kept, staged, landed,
     to_ref, from_ref, load_sem, send_sem, recv_sem_a, recv_sem_b, back_send_sem, back_recv_sem,
 ):
     me = lax.axis_index("pb")
 
     loads = [
-        pltpu.make_async_copy(x_hbm.at[pl.ds(16, 16), pl.ds(0, 384)], xin.at[pl.ds(16, 16), pl.ds(0, 384)], load_sem.at[0]),
-        pltpu.make_async_copy(x_hbm.at[pl.ds(16, 16), pl.ds(384, 816)], xin.at[pl.ds(16, 16), pl.ds(384, 816)], load_sem.at[1]),
+        pltpu.make_async_copy(x_hbm.at[pl.ds(16, 16), pl.ds(0, FIRST)], xin.at[pl.ds(16, 16), pl.ds(0, FIRST)], load_sem.at[0]),
+        pltpu.make_async_copy(x_hbm.at[pl.ds(16, 16), pl.ds(FIRST, NG - FIRST)], xin.at[pl.ds(16, 16), pl.ds(FIRST, NG - FIRST)], load_sem.at[1]),
         pltpu.make_async_copy(x_hbm.at[pl.ds(0, 16), pl.ds(MAIN, TAIL)], xin.at[pl.ds(0, 16), pl.ds(MAIN, TAIL)], load_sem.at[2]),
         pltpu.make_async_copy(x_hbm.at[pl.ds(0, 16), pl.ds(0, MAIN)], xin.at[pl.ds(0, 16), pl.ds(0, MAIN)], load_sem.at[3]),
         pltpu.make_async_copy(w_hbm, w_in, load_sem.at[4]),
+        pltpu.make_async_copy(live_hbm, live_ref, load_sem.at[5]),
     ]
     for load in loads:
         load.start()
 
+    recv_t[...] = jnp.zeros_like(recv_t)
     barrier = pltpu.get_barrier_semaphore()
 
     def greet(slot, _):
         pl.semaphore_signal(barrier, inc=1, device_id=(lax.rem(me + slot, DEV),), device_id_type=MESH)
         return 0
 
-    lax.fori_loop(1, DEV, greet, 0)
+    for i in range(1, DEV):
+        greet(i, 0)
 
     fill_places(me, to_ref, from_ref)
 
@@ -94,62 +99,86 @@
             turn[slot, :, r, :] = turned(xin[first_row + r, pl.ds(column, 128), :])
         out[:, :, pl.ds(out_column, 128)] = turn[slot].astype(BF16)
 
-    def turn_blocks(first_row, begin, end, out):
+    def turn_blocks(first_row, begin, end, out, left_out):
         def body(j, _):
             column = pl.multiple_of(j * 128, 128)
-            turn_block(first_row, column, lax.rem(j, 2), out, column)
+            turn_block(first_row, column, lax.rem(j, 2), out, pl.multiple_of(column - left_out, 128))
             return 0
 
         lax.fori_loop(begin, end, body, 0)
 
-    def send_part(src, dst, begin, width, sem_s, sem_r, group):
+    def send_part(src, dst, sem_s, sem_r, group, rows=PAIRS):
+        rows = pl.ds(0, rows)
+
         def body(slot, _):
             to = to_ref[slot]
             pltpu.make_async_remote_copy(
-                src.at[to, :, pl.ds(begin, width)],
-                dst.at[slot, :, pl.ds(begin, width)],
-                sem_s,
-                sem_r.at[lax.div(slot, group)],
-                device_id=(to,),
-                device_id_type=MESH,
+                src.at[to, rows], dst.at[slot, rows], sem_s, sem_r.at[lax.div(slot, group)],
+                device_id=(to,), device_id_type=MESH,
             ).start()
             return 0
 
         lax.fori_loop(1, DEV, body, 0)
-        pltpu.make_async_copy(
-            src.at[me, :, pl.ds(begin, width)], dst.at[0, :, pl.ds(begin, width)], sem_r.at[0]
-        ).start()
-
-    (a0, a1), (_, a2) = PARTS_A
+        pltpu.make_async_copy(src.at[me, rows], dst.at[0, rows], sem_r.at[0]).start()
+
     loads[0].wait()
-    turn_blocks(16, 0, 3, send_a)
+    turn_blocks(16, 0, FIRST // 128, send_a, 0)
     pl.semaphore_wait(barrier, DEV - 1)
-    send_part(send_a, recv_a, a0, a1 - a0, send_sem.at[0], recv_sem_a.at[0], GROUP)
+    send_part(send_a, recv_a, send_sem.at[0], recv_sem_a.at[0], GROUP)
     loads[1].wait()
     loads[2].wait()
-    turn_blocks(16, 3, 9, send_a)
-    for r in range(PAIRS):
-        gap = jnp.zeros((HALF - TAIL, 128), BF16)
-        both = [xin[16 + r, MAIN:NG, :], gap, xin[r, MAIN:NG, :], gap]
+    turn_blocks(16, FIRST // 128, 9, send_m, FIRST)
+    send_part(send_m, recv_m, send_sem.at[1], recv_sem_a.at[1], GROUP)
+
+    def tail_rows(r, begin, end):
+        rows = [xin[PAIRS + r, MAIN + begin : MAIN + min(end, TAIL), :]] if begin < TAIL else []
+        if end > TAIL:
+            rows.append(xin[r, MAIN + max(begin - TAIL, 0) : MAIN + end - TAIL, :])
+        return rows
+
+    for r in range(FULL):
+        begin = r % 3 * THIRD
+        both = tail_rows(r, 0, 2 * TAIL) + tail_rows(FULL + r // 3, begin, begin + THIRD)
         turn[1, :, r, :] = turned(jnp.concatenate(both, axis=0))
-    send_a[:, :, MAIN:LANES_A] = turn[1].astype(BF16)
-    send_part(send_a, recv_a, a1, a2 - a1, send_sem.at[1], recv_sem_a.at[1], GROUP)
+    send_t[...] = turn[1].astype(BF16)
+    send_part(send_t, recv_t, send_sem.at[3], recv_sem_a.at[2], GROUP, FULL)
     loads[3].wait()
-    turn_blocks(0, 0, 9, send_b)
-    send_part(send_b, recv_b, 0, LANES_B, send_sem.at[2], recv_sem_b, FEW)
+    turn_blocks(0, 0, 9, send_b, 0)
+    send_part(send_b, recv_b, send_sem.at[2], recv_sem_b, FEW)
 
     loads[4].wait()
     w_wide[...] = jnp.zeros_like(w_wide)
-    w_wide[pl.ds(HALF, TAIL), pl.ds(0, NG)] = w_in[pl.ds(MAIN, TAIL), :]
+    w_wide[pl.ds(TAIL, TAIL), pl.ds(0, NG)] = w_in[pl.ds(MAIN, TAIL), :]
     w_wide[pl.ds(128, MAIN), pl.ds(0, NG)] = w_in[pl.ds(0, MAIN), :]
     spread[...] = same_block((ROWS, 256), 1, 16, 1, 16).astype(BF16)
 
+    row = lax.broadcasted_iota(jnp.int32, (256, 256), 0)
+    col = lax.broadcasted_iota(jnp.int32, (256, 256), 1)
+    lane = lax.broadcasted_iota(jnp.int32, (128, 128), 0)
+    goal = lax.broadcasted_iota(jnp.int32, (128, 128), 1)
+    for c in range(3):
+        same = (row // PAIRS == col // PAIRS) & (row % PAIRS >= FULL) & ((row % PAIRS - FULL) * 3 + c == col % PAIRS)
+        lift[c] = same.astype(F32).astype(BF16)
+        moved = (lane >= 2 * TAIL) & (lane - 2 * TAIL + c * THIRD == goal)
+        shift[c] = moved.astype(F32).astype(BF16)
+
+    def whole_tails(travelled):
+        own = lax.broadcasted_iota(jnp.int32, (256, 128), 1) < 2 * TAIL
+        total = jnp.where(own, travelled.astype(F32), 0.0)
+        for c in range(3):
+            third = jnp.dot(lift[c], travelled, preferred_element_type=F32).astype(BF16)
+            total = total + jnp.dot(third, shift[c], preferred_element_type=F32)
+        return total.astype(BF16)
+
     def screen(g, _):
         slots = pl.ds(g * GROUP, GROUP)
-        for p, (begin, end) in enumerate(PARTS_A):
-            view = recv_a.at[slots, :, pl.ds(begin, end - begin)]
+        for p, (part, rows) in enumerate(((recv_a, PAIRS), (recv_m, PAIRS), (recv_t, FULL))):
+            view = part.at[slots, pl.ds(0, rows)]
             pltpu.make_async_copy(view, view, recv_sem_a.at[p, g]).wait()
-        left = recv_a[slots].reshape(GROUP * PAIRS, LANES_A)
+        tail = whole_tails(recv_t[slots].reshape(GROUP * PAIRS, 128))
+        tails[pl.ds(g * GROUP * PAIRS, GROUP * PAIRS), :] = tail
+        main = jnp.concatenate([recv_a[slots], recv_m[slots]], axis=2).reshape(GROUP * PAIRS, MAIN)
+        left = jnp.concatenate([main, tail], axis=1)
 
         def column(n, _):
             rows = pl.ds(pl.multiple_of(n * 256, 256), 256)
@@ -165,9 +194,8 @@
     def contract(g, _):
         slots = pl.ds(g * FEW, FEW)
         nt = (((1,), (1,)), ((), ()))
-        tails = recv_a[slots, :, MAIN:LANES_A].reshape(ROWS, 128)
         right = screened[pl.ds(g * ROWS, ROWS), :]
-        early = lax.dot_general(tails, right[:, :128], nt, preferred_element_type=F32)
+        early = lax.dot_general(tails[pl.ds(g * ROWS, ROWS), :], right[:, :128], nt, preferred_element_type=F32)
         view = recv_b.at[slots]
         pltpu.make_async_copy(view, view, recv_sem_b.at[g]).wait()
         mains = recv_b[slots].reshape(ROWS, MAIN)
@@ -196,6 +224,7 @@
             give_back(i, 0)
         return 0
 
+    loads[5].wait()
     ones = jnp.ones((DEV, 128), BF16)
     diagonal = jnp.where(same_block((DEV, DEV), 1, DEV, 1, DEV), live_ref[...].astype(F32), 0.0).astype(BF16)
     kept[...] = jnp.dot(diagonal, ones, preferred_element_type=F32)
@@ -203,11 +232,9 @@
     lax.fori_loop(0, FEWS, contract, 0)
     pltpu.make_async_copy(staged.at[0], landed.at[me], back_recv_sem).start()
 
-    for p, (begin, end) in enumerate(PARTS_A):
-        view = send_a.at[pl.ds(1, DEV - 1), :, pl.ds(begin, end - begin)]
+    for p, (part, rows) in enumerate(((send_a, PAIRS), (send_m, PAIRS), (send_b, PAIRS), (send_t, FULL))):
+        view = part.at[pl.ds(1, DEV - 1), pl.ds(0, rows)]
         pltpu.make_async_copy(view, view, send_sem.at[p]).wait()
-    view = send_b.at[pl.ds(1, DEV - 1)]
-    pltpu.make_async_copy(view, view, send_sem.at[2]).wait()
     view = staged.at[pl.ds(1, DEV - 1)]
     pltpu.make_async_copy(view, view, back_send_sem).wait()
     pltpu.make_async_copy(landed, landed, back_recv_sem).wait()
@@ -220,27 +247,35 @@
     blocks = pl.pallas_call(
         kernel,
         out_shape=jax.ShapeDtypeStruct((DEV, PAIRS * PAIRS), BF16),
-        in_specs=[pl.BlockSpec(memory_space=pltpu.HBM)] * 2 + [pl.BlockSpec(memory_space=pltpu.VMEM)],
+        in_specs=[pl.BlockSpec(memory_space=pltpu.HBM)] * 3,
         out_specs=pl.BlockSpec(memory_space=pltpu.VMEM),
         scratch_shapes=[
             pltpu.VMEM((2 * PAIRS, NG, DEV), BF16),
             pltpu.VMEM((NG, NG), BF16),
             pltpu.VMEM((LANES_A, LANES_A), BF16),
-            pltpu.VMEM((DEV, PAIRS, LANES_A), BF16),
+            pltpu.VMEM((DEV, PAIRS, FIRST), BF16),
+            pltpu.VMEM((DEV, PAIRS, REST), BF16),
+            pltpu.VMEM((DEV, PAIRS, 128), BF16),
             pltpu.VMEM((DEV, PAIRS, LANES_B), BF16),
-            pltpu.VMEM((DEV, PAIRS, LANES_A), BF16),
+            pltpu.VMEM((DEV, PAIRS, FIRST), BF16),
+            pltpu.VMEM((DEV, PAIRS, REST), BF16),
+            pltpu.VMEM((DEV, PAIRS, 128), BF16),
             pltpu.VMEM((DEV, PAIRS, LANES_B), BF16),
+            pltpu.VMEM((DEV * PAIRS, 128), BF16),
+            pltpu.VMEM((3, 256, 256), BF16),
+            pltpu.VMEM((3, 128, 128), BF16),
             pltpu.VMEM((DEV * PAIRS, LANES_A), BF16),
             pltpu.VMEM((2, DEV, PAIRS, 128), F32),
             pltpu.VMEM((ROWS, 256), BF16),
+            pltpu.VMEM((1, DEV), jnp.int32),
             pltpu.VMEM((DEV, 128), F32),
             pltpu.VMEM((DEV, 2, 128), F32),
             pltpu.VMEM((DEV, 2, 128), F32),
             pltpu.SMEM((DEV,), jnp.int32),
             pltpu.SMEM((DEV,), jnp.int32),
-            pltpu.SemaphoreType.DMA((5,)),
-            pltpu.SemaphoreType.DMA((3,)),
-            pltpu.SemaphoreType.DMA((2, GROUPS)),
+            pltpu.SemaphoreType.DMA((6,)),
+            pltpu.SemaphoreType.DMA((4,)),
+            pltpu.SemaphoreType.DMA((3, GROUPS)),
             pltpu.SemaphoreType.DMA((FEWS,)),
             pltpu.SemaphoreType.DMA,
             pltpu.SemaphoreType.DMA,
@@ -248,7 +283,7 @@
         compiler_params=pltpu.CompilerParams(
             collective_id=0, has_side_effects=True, vmem_limit_bytes=52 << 20
         ),
-    )(x, screening[0], live.reshape(1, DEV))
+    )(x, screening[0], pltpu.with_memory_space_constraint(live.reshape(1, DEV), pltpu.HBM))
     return blocks[:, None, :]
 
 

time: 127 us -> 125 us (0.984)
  Pallas kernels: 126 us -> 124 us
    pallas_call x1, Pallas kernels: 126 us -> 124 us  [on_device(): pl.pallas_call(kernel, out_shape=jax.ShapeDtypeStruct((DEV, PAIRS * PAIRS...]
where the time goes in v4:
time: 125 us
  Pallas kernels  124 us (99%)
    pallas_call x1, Pallas kernels, on_device(): pl.pallas_call(kernel, out_shape=jax.ShapeDtypeStruct((DEV, PAIRS * PAIRS...  124 us

profile of v4, /device:TPU:1, one launch (start us, length us, event | category | flops | bytes accessed | tf_op | source)
XLA Modules:
  0.0 124.8 jit_solution(10679760326412777029)
XLA Ops:
  0.0 124.2 %shard_map.37 = bf16[128,256]{1,0:T(8,128)(2,1)S(1)} custom-call(bf16[32,1200,128]{2,1,0:T(8,128)(2,1)} %bitcast.7, bf16[1200,1200]{1,0:T(8,128)(2,1)} %bitcast.8, s32[1,128]{1,0:T(1,128)} %bitcast.9), custom_call_target="tpu_custom_call" | custom-call | tf_op jit(solution)/shard_map/pallas_call | solution.py:247
  124.2 0.6 copy.5

commit v5 on v4

v5 whole, which is shorter than its diff:
```python
import jax
import jax.numpy as jnp
from jax import lax
from jax.experimental import pallas as pl
from jax.experimental.pallas import tpu as pltpu
from jax.sharding import PartitionSpec as P

F32 = jnp.float32
BF16 = jnp.bfloat16
MESH = pl.DeviceIdType.MESH

DEV = 128
PAIRS = 16
NG = 1200
MAIN = 1152
TAIL = NG - MAIN
LANES_A = MAIN + 128
HALF = PAIRS // 2
LANES_B = MAIN
STEP = 37
GROUP = 16
GROUPS = DEV // GROUP
FEW = 8
FEWS = DEV // FEW
ROWS = FEW * PAIRS
FIRST = 384
REST = MAIN - FIRST


def digits(i):
    return i // 32, i // 8 % 4, i // 2 % 4, i % 2


def hops(i):
    return sum(min(d, 4 - d) for d in digits(i)[:3])


_MIXED = [i * STEP % DEV for i in range(1, DEV)]
ORDER = [0] + sorted(_MIXED, key=lambda i: hops(i) <= 1)


def fill_places(me, to_ref, from_ref):
    z, x, y, c = lax.div(me, 32), lax.rem(lax.div(me, 8), 4), lax.rem(lax.div(me, 2), 4), lax.rem(me, 2)
    at = [
        [lax.rem(own + d, size) * unit for d in range(size)]
        for own, size, unit in ((z, 4, 32), (x, 4, 8), (y, 4, 2), (c, 2, 1))
    ]
    for slot, offset in enumerate(ORDER):
        there = digits(offset)
        back = [-d % size for d, size in zip(there, (4, 4, 4, 2))]
        to_ref[slot] = sum(column[d] for column, d in zip(at, there))
        from_ref[slot] = sum(column[d] for column, d in zip(at, back))


def same_block(shape, div0, mod0, div1, mod1):
    row = lax.broadcasted_iota(jnp.int32, shape, 0)
    col = lax.broadcasted_iota(jnp.int32, shape, 1)
    row = row // div0 if div0 > 1 else row % mod0
    col = col // div1 if div1 > 1 else col % mod1
    return row == col


def kernel(
    x_hbm, w_hbm, live_hbm, o_ref,
    xin, w_in, w_wide, send_a, send_m, send_t, recv_a, recv_m, recv_t, own_main, own_tail,
    screened, screened_t, recv_s, recv_st, turn, spread, live_ref, kept, landed,
    to_ref, from_ref, load_sem, send_sem, recv_sem_a, recv_sem_s,
):
    me = lax.axis_index("pb")

    loads = [
        pltpu.make_async_copy(x_hbm.at[pl.ds(16, 16), pl.ds(0, FIRST)], xin.at[pl.ds(16, 16), pl.ds(0, FIRST)], load_sem.at[0]),
        pltpu.make_async_copy(x_hbm.at[pl.ds(16, 16), pl.ds(FIRST, NG - FIRST)], xin.at[pl.ds(16, 16), pl.ds(FIRST, NG - FIRST)], load_sem.at[1]),
        pltpu.make_async_copy(x_hbm.at[pl.ds(0, 16), pl.ds(MAIN, TAIL)], xin.at[pl.ds(0, 16), pl.ds(MAIN, TAIL)], load_sem.at[2]),
        pltpu.make_async_copy(x_hbm.at[pl.ds(0, 16), pl.ds(0, MAIN)], xin.at[pl.ds(0, 16), pl.ds(0, MAIN)], load_sem.at[3]),
        pltpu.make_async_copy(w_hbm, w_in, load_sem.at[4]),
        pltpu.make_async_copy(live_hbm, live_ref, load_sem.at[5]),
    ]
    for load in loads:
        load.start()

    barrier = pltpu.get_barrier_semaphore()

    def greet(slot, _):
        pl.semaphore_signal(barrier, inc=1, device_id=(lax.rem(me + slot, DEV),), device_id_type=MESH)
        return 0

    for i in range(1, DEV):
        greet(i, 0)

    fill_places(me, to_ref, from_ref)

    def turned(block):
        return jnp.transpose(block).astype(F32)

    def turn_block(first_row, column, slot, out, out_column):
        for r in range(PAIRS):
            turn[slot, :, r, :] = turned(xin[first_row + r, pl.ds(column, 128), :])
        out[:, :, pl.ds(out_column, 128)] = turn[slot].astype(BF16)

    def turn_blocks(first_row, begin, end, out, left_out):
        def body(j, _):
            column = pl.multiple_of(j * 128, 128)
            turn_block(first_row, column, lax.rem(j, 2), out, pl.multiple_of(column - left_out, 128))
            return 0

        lax.fori_loop(begin, end, body, 0)

    def send_part(src, dst, sem_s, sem_r, group):

        def body(slot, _):
            to = to_ref[slot]
            pltpu.make_async_remote_copy(
                src.at[to], dst.at[slot], sem_s, sem_r.at[lax.div(slot, group)],
                device_id=(to,), device_id_type=MESH,
            ).start()
            return 0

        lax.fori_loop(1, DEV, body, 0)
        pltpu.make_async_copy(src.at[me], dst.at[0], sem_r.at[0]).start()

    loads[0].wait()
    turn_blocks(16, 0, FIRST // 128, send_a, 0)
    pl.semaphore_wait(barrier, DEV - 1)
    send_part(send_a, recv_a, send_sem.at[0], recv_sem_a.at[0], GROUP)
    loads[1].wait()
    loads[2].wait()

    for r in range(HALF):
        gap = jnp.zeros((128 - 2 * TAIL, 128), BF16)
        both = [xin[PAIRS + r, MAIN:NG, :], xin[PAIRS + HALF + r, MAIN:NG, :], gap]
        turn[1, :, r, :] = turned(jnp.concatenate(both, axis=0))
    send_t[...] = turn[1, :, :HALF, :].astype(BF16)
    send_part(send_t, recv_t, send_sem.at[2], recv_sem_a.at[2], GROUP)
    turn_blocks(16, FIRST // 128, 9, send_m, FIRST)
    send_part(send_m, recv_m, send_sem.at[1], recv_sem_a.at[1], GROUP)

    loads[3].wait()
    turn_blocks(0, 0, 9, own_main, 0)
    for r in range(PAIRS):
        gap = jnp.zeros((128 - 2 * TAIL, 128), BF16)
        both = [xin[r, MAIN:NG, :], xin[r, MAIN:NG, :], gap]
        turn[1, :, r, :] = turned(jnp.concatenate(both, axis=0))
    own_tail[...] = turn[1].astype(BF16)

    loads[4].wait()
    lane = lax.broadcasted_iota(jnp.int32, (TAIL, 128), 1)
    line = lax.broadcasted_iota(jnp.int32, (TAIL, 128), 0)
    twice = ((lane == line) | (lane == line + TAIL)).astype(F32).astype(BF16)
    w_wide[...] = jnp.zeros_like(w_wide)
    for row, first, count in ((0, MAIN, TAIL), (TAIL, MAIN, TAIL), (128, 0, MAIN)):
        w_wide[pl.ds(row, count), pl.ds(0, MAIN)] = w_in[pl.ds(first, count), pl.ds(0, MAIN)]
        ends = jnp.dot(w_in[pl.ds(first, count), pl.ds(MAIN, TAIL)], twice, preferred_element_type=F32)
        w_wide[pl.ds(row, count), pl.ds(MAIN, 128)] = ends.astype(BF16)
    spread[...] = same_block((ROWS, 256), 1, 16, 1, 16).astype(BF16)

    def pairing(slots):
        tall = lax.broadcasted_iota(jnp.int32, (slots * PAIRS, slots * HALF), 0)
        low = lax.broadcasted_iota(jnp.int32, (slots * PAIRS, slots * HALF), 1)
        pick = (tall // PAIRS == low // HALF) & (tall % HALF == low % HALF)
        b = lax.broadcasted_iota(jnp.int32, (slots * PAIRS, 128), 0) % PAIRS // HALF
        lane = lax.broadcasted_iota(jnp.int32, (slots * PAIRS, 128), 1) // TAIL
        return pick.astype(F32).astype(BF16), lane == b

    def apart(packed, slots):
        pick, held = pairing(slots)
        rows = jnp.dot(pick, packed, preferred_element_type=F32)
        return jnp.where(held, rows, 0.0).astype(BF16)

    def together(rows, slots):
        pick, held = pairing(slots)
        rows = jnp.where(held, rows, 0.0).astype(BF16)
        return lax.dot_general(pick, rows, (((0,), (0,)), ((), ())), preferred_element_type=F32).astype(BF16)

    nt = (((1,), (1,)), ((), ()))

    def screen(g, _):
        slots = pl.ds(g * GROUP, GROUP)
        for p, part in enumerate((recv_a, recv_m, recv_t)):
            view = part.at[slots]
            pltpu.make_async_copy(view, view, recv_sem_a.at[p, g]).wait()
        tail = apart(recv_t[slots].reshape(GROUP * HALF, 128), GROUP)
        main = jnp.concatenate([recv_a[slots], recv_m[slots]], axis=2).reshape(GROUP * PAIRS, MAIN)
        left = jnp.concatenate([main, tail], axis=1)
        ends = lax.dot_general(left, w_wide[pl.ds(0, 128), :], nt, preferred_element_type=F32)
        screened_t[slots] = together(ends, GROUP).reshape(GROUP, HALF, 128)

        def column(n, _):
            rows = pl.ds(pl.multiple_of(128 + n * 384, 128), 384)
            part = lax.dot_general(left, w_wide[rows, :], nt, preferred_element_type=F32)
            lanes = pl.ds(pl.multiple_of(n * 384, 128), 384)
            screened[slots, :, lanes] = part.astype(BF16).reshape(GROUP, PAIRS, 384)
            return 0

        lax.fori_loop(0, 3, column, 0)

        def pass_on(slot, _):
            to = from_ref[slot]
            for p, (src, dst) in enumerate(((screened, recv_s), (screened_t, recv_st))):
                pltpu.make_async_remote_copy(
                    src.at[slot], dst.at[slot], send_sem.at[3 + p], recv_sem_s.at[p, lax.div(slot, FEW)],
                    device_id=(to,), device_id_type=MESH,
                ).start()
            return 0

        @pl.when(g == 0)
        def _():
            for p, (src, dst) in enumerate(((screened, recv_s), (screened_t, recv_st))):
                pltpu.make_async_copy(src.at[0], dst.at[0], recv_sem_s.at[p, 0]).start()

        lax.fori_loop(jnp.where(g == 0, 1, g * GROUP), g * GROUP + GROUP, pass_on, 0)
        return 0

    lax.fori_loop(0, GROUPS, screen, 0)

    def contract(g, _):
        slots = pl.ds(g * FEW, FEW)
        places = [to_ref[g * FEW + i] for i in range(FEW)]
        mains = jnp.concatenate([own_main[q] for q in places], axis=0)
        tails = jnp.concatenate([own_tail[q] for q in places], axis=0)
        for p, part in enumerate((recv_s, recv_st)):
            view = part.at[slots]
            pltpu.make_async_copy(view, view, recv_sem_s.at[p, g]).wait()
        ends = apart(recv_st[slots].reshape(FEW * HALF, 128), FEW)
        every = lax.dot_general(mains, recv_s[slots].reshape(ROWS, MAIN), nt, preferred_element_type=F32)
        every = every + lax.dot_general(tails, ends, nt, preferred_element_type=F32)
        own = jnp.where(same_block((ROWS, ROWS), 16, 0, 16, 0), every, 0.0).astype(BF16)
        wide = jnp.dot(own, spread[...], preferred_element_type=F32)
        wide = jnp.where(same_block((ROWS, 256), 1, 16, 16, 0), wide, 0.0).astype(BF16)
        gather = same_block((FEW, ROWS), 1, FEW, 16, 0).astype(BF16)
        rows = jnp.dot(gather, wide, preferred_element_type=F32)
        for i, q in enumerate(places):
            landed[q, 0:1, :] = rows[i : i + 1, :128]
            landed[q, 1:2, :] = rows[i : i + 1, 128:]
        return 0

    loads[5].wait()
    ones = jnp.ones((DEV, 128), BF16)
    diagonal = jnp.where(same_block((DEV, DEV), 1, DEV, 1, DEV), live_ref[...].astype(F32), 0.0).astype(BF16)
    kept[...] = jnp.dot(diagonal, ones, preferred_element_type=F32)

    lax.fori_loop(0, FEWS, contract, 0)

    for p, part in enumerate((send_a, send_m, send_t, screened, screened_t)):
        view = part.at[pl.ds(1, DEV - 1)]
        pltpu.make_async_copy(view, view, send_sem.at[p]).wait()
    o_ref[:, :128] = (landed[:, 0, :] * kept[...]).astype(BF16)
    o_ref[:, 128:] = (landed[:, 1, :] * kept[...]).astype(BF16)


def on_device(densities, screening, live):
    x = jnp.transpose(densities, (1, 2, 3, 0))[0]
    blocks = pl.pallas_call(
        kernel,
        out_shape=jax.ShapeDtypeStruct((DEV, PAIRS * PAIRS), BF16),
        in_specs=[pl.BlockSpec(memory_space=pltpu.HBM)] * 3,
        out_specs=pl.BlockSpec(memory_space=pltpu.VMEM),
        scratch_shapes=[
            pltpu.VMEM((2 * PAIRS, NG, DEV), BF16),
            pltpu.VMEM((NG, NG), BF16),
            pltpu.VMEM((LANES_A, LANES_A), BF16),
            pltpu.VMEM((DEV, PAIRS, FIRST), BF16),
            pltpu.VMEM((DEV, PAIRS, REST), BF16),
            pltpu.VMEM((DEV, HALF, 128), BF16),
            pltpu.VMEM((DEV, PAIRS, FIRST), BF16),
            pltpu.VMEM((DEV, PAIRS, REST), BF16),
            pltpu.VMEM((DEV, HALF, 128), BF16),
            pltpu.VMEM((DEV, PAIRS, MAIN), BF16),
            pltpu.VMEM((DEV, PAIRS, 128), BF16),
            pltpu.VMEM((DEV, PAIRS, MAIN), BF16),
            pltpu.VMEM((DEV, HALF, 128), BF16),
            pltpu.VMEM((DEV, PAIRS, MAIN), BF16),
            pltpu.VMEM((DEV, HALF, 128), BF16),
            pltpu.VMEM((2, DEV, PAIRS, 128), F32),
            pltpu.VMEM((ROWS, 256), BF16),
            pltpu.VMEM((1, DEV), jnp.int32),
            pltpu.VMEM((DEV, 128), F32),
            pltpu.VMEM((DEV, 2, 128), F32),
            pltpu.SMEM((DEV,), jnp.int32),
            pltpu.SMEM((DEV,), jnp.int32),
            pltpu.SemaphoreType.DMA((6,)),
            pltpu.SemaphoreType.DMA((5,)),
            pltpu.SemaphoreType.DMA((3, GROUPS)),
            pltpu.SemaphoreType.DMA((2, FEWS)),
        ],
        compiler_params=pltpu.CompilerParams(
            collective_id=0, has_side_effects=True, vmem_limit_bytes=52 << 20
        ),
    )(x, screening[0], pltpu.with_memory_space_constraint(live.reshape(1, DEV), pltpu.HBM))
    return blocks[:, None, :]


def solution(mesh):
    in_specs = (P(None, "pb", None, None), P("pb", None, None), P(None, "pb"))
    return jax.shard_map(
        on_device, mesh=mesh, in_specs=in_specs, out_specs=P(None, "pb", None), check_vma=False
    )
```

time: 125 us -> 123 us (0.984)
  Pallas kernels: 124 us -> 122 us
    pallas_call x1, Pallas kernels: 124 us -> 122 us  [on_device(): pl.pallas_call(kernel, out_shape=jax.ShapeDtypeStruct((DEV, PAIRS * PAIRS...]
where the time goes in v5:
time: 123 us
  Pallas kernels  122 us (99%)
    pallas_call x1, Pallas kernels, on_device(): pl.pallas_call(kernel, out_shape=jax.ShapeDtypeStruct((DEV, PAIRS * PAIRS...  122 us

profile of v5, /device:TPU:1, one launch (start us, length us, event | category | flops | bytes accessed | tf_op | source)
XLA Modules:
  0.0 122.8 jit_solution(7845330184993085368)
XLA Ops:
  0.0 122.1 %shard_map.37 = bf16[128,256]{1,0:T(8,128)(2,1)S(1)} custom-call(bf16[32,1200,128]{2,1,0:T(8,128)(2,1)} %bitcast.7, bf16[1200,1200]{1,0:T(8,128)(2,1)} %bitcast.8, s32[1,128]{1,0:T(1,128)} %bitcast.9), custom_call_target="tpu_custom_call" | custom-call | tf_op jit(solution)/shard_map/pallas_call | solution.py:253
  122.2 0.6 copy.5

commit v6 on v5

--- a/solution.py
+++ b/solution.py
@@ -20,7 +20,7 @@
 STEP = 37
 GROUP = 16
 GROUPS = DEV // GROUP
-FEW = 8
+FEW = 16
 FEWS = DEV // FEW
 ROWS = FEW * PAIRS
 FIRST = 384
@@ -63,7 +63,7 @@
 def kernel(
     x_hbm, w_hbm, live_hbm, o_ref,
     xin, w_in, w_wide, send_a, send_m, send_t, recv_a, recv_m, recv_t, own_main, own_tail,
-    screened, screened_t, recv_s, recv_st, turn, spread, live_ref, kept, landed,
+    screened, screened_t, recv_s, recv_st, turn, spread, same_q, same_a, gather, pick, held, live_ref, kept, landed,
     to_ref, from_ref, load_sem, send_sem, recv_sem_a, recv_sem_s,
 ):
     me = lax.axis_index("pb")
@@ -154,23 +154,22 @@
         w_wide[pl.ds(row, count), pl.ds(MAIN, 128)] = ends.astype(BF16)
     spread[...] = same_block((ROWS, 256), 1, 16, 1, 16).astype(BF16)
 
-    def pairing(slots):
-        tall = lax.broadcasted_iota(jnp.int32, (slots * PAIRS, slots * HALF), 0)
-        low = lax.broadcasted_iota(jnp.int32, (slots * PAIRS, slots * HALF), 1)
-        pick = (tall // PAIRS == low // HALF) & (tall % HALF == low % HALF)
-        b = lax.broadcasted_iota(jnp.int32, (slots * PAIRS, 128), 0) % PAIRS // HALF
-        lane = lax.broadcasted_iota(jnp.int32, (slots * PAIRS, 128), 1) // TAIL
-        return pick.astype(F32).astype(BF16), lane == b
-
-    def apart(packed, slots):
-        pick, held = pairing(slots)
-        rows = jnp.dot(pick, packed, preferred_element_type=F32)
-        return jnp.where(held, rows, 0.0).astype(BF16)
-
-    def together(rows, slots):
-        pick, held = pairing(slots)
-        rows = jnp.where(held, rows, 0.0).astype(BF16)
-        return lax.dot_general(pick, rows, (((0,), (0,)), ((), ())), preferred_element_type=F32).astype(BF16)
+    same_q[...] = same_block((ROWS, ROWS), 16, 0, 16, 0).astype(F32)
+    same_a[...] = same_block((ROWS, 256), 1, 16, 16, 0).astype(F32)
+    gather[...] = same_block((FEW, ROWS), 1, FEW, 16, 0).astype(BF16)
+    tall = lax.broadcasted_iota(jnp.int32, (ROWS, FEW * HALF), 0)
+    low = lax.broadcasted_iota(jnp.int32, (ROWS, FEW * HALF), 1)
+    pick[...] = ((tall // PAIRS == low // HALF) & (tall % HALF == low % HALF)).astype(F32).astype(BF16)
+    half = lax.broadcasted_iota(jnp.int32, (ROWS, 128), 0) % PAIRS // HALF
+    held[...] = (lax.broadcasted_iota(jnp.int32, (ROWS, 128), 1) // TAIL == half).astype(F32)
+
+    def apart(packed):
+        rows = jnp.dot(pick[...], packed, preferred_element_type=F32)
+        return (rows * held[...]).astype(BF16)
+
+    def together(rows):
+        rows = (rows * held[...]).astype(BF16)
+        return lax.dot_general(pick[...], rows, (((0,), (0,)), ((), ())), preferred_element_type=F32).astype(BF16)
 
     nt = (((1,), (1,)), ((), ()))
 
@@ -179,11 +178,11 @@
         for p, part in enumerate((recv_a, recv_m, recv_t)):
             view = part.at[slots]
             pltpu.make_async_copy(view, view, recv_sem_a.at[p, g]).wait()
-        tail = apart(recv_t[slots].reshape(GROUP * HALF, 128), GROUP)
+        tail = apart(recv_t[slots].reshape(GROUP * HALF, 128))
         main = jnp.concatenate([recv_a[slots], recv_m[slots]], axis=2).reshape(GROUP * PAIRS, MAIN)
         left = jnp.concatenate([main, tail], axis=1)
         ends = lax.dot_general(left, w_wide[pl.ds(0, 128), :], nt, preferred_element_type=F32)
-        screened_t[slots] = together(ends, GROUP).reshape(GROUP, HALF, 128)
+        screened_t[slots] = together(ends).reshape(GROUP, HALF, 128)
 
         def column(n, _):
             rows = pl.ds(pl.multiple_of(128 + n * 384, 128), 384)
@@ -221,14 +220,13 @@
         for p, part in enumerate((recv_s, recv_st)):
             view = part.at[slots]
             pltpu.make_async_copy(view, view, recv_sem_s.at[p, g]).wait()
-        ends = apart(recv_st[slots].reshape(FEW * HALF, 128), FEW)
+        ends = apart(recv_st[slots].reshape(FEW * HALF, 128))
         every = lax.dot_general(mains, recv_s[slots].reshape(ROWS, MAIN), nt, preferred_element_type=F32)
         every = every + lax.dot_general(tails, ends, nt, preferred_element_type=F32)
-        own = jnp.where(same_block((ROWS, ROWS), 16, 0, 16, 0), every, 0.0).astype(BF16)
+        own = (every * same_q[...]).astype(BF16)
         wide = jnp.dot(own, spread[...], preferred_element_type=F32)
-        wide = jnp.where(same_block((ROWS, 256), 1, 16, 16, 0), wide, 0.0).astype(BF16)
-        gather = same_block((FEW, ROWS), 1, FEW, 16, 0).astype(BF16)
-        rows = jnp.dot(gather, wide, preferred_element_type=F32)
+        wide = (wide * same_a[...]).astype(BF16)
+        rows = jnp.dot(gather[...], wide, preferred_element_type=F32)
         for i, q in enumerate(places):
             landed[q, 0:1, :] = rows[i : i + 1, :128]
             landed[q, 1:2, :] = rows[i : i + 1, 128:]
@@ -273,6 +271,11 @@
             pltpu.VMEM((DEV, HALF, 128), BF16),
             pltpu.VMEM((2, DEV, PAIRS, 128), F32),
             pltpu.VMEM((ROWS, 256), BF16),
+            pltpu.VMEM((ROWS, ROWS), F32),
+            pltpu.VMEM((ROWS, 256), F32),
+            pltpu.VMEM((FEW, ROWS), BF16),
+            pltpu.VMEM((ROWS, FEW * HALF), BF16),
+            pltpu.VMEM((ROWS, 128), F32),
             pltpu.VMEM((1, DEV), jnp.int32),
             pltpu.VMEM((DEV, 128), F32),
             pltpu.VMEM((DEV, 2, 128), F32),

time: 123 us -> 123 us (level)
  no operation moved by 1% of the time
where the time goes in v6:
time: 123 us
  Pallas kernels  122 us (99%)
    pallas_call x1, Pallas kernels, on_device(): pl.pallas_call(kernel, out_shape=jax.ShapeDtypeStruct((DEV, PAIRS * PAIRS...  122 us

profile of v6, /device:TPU:1, one launch (start us, length us, event | category | flops | bytes accessed | tf_op | source)
XLA Modules:
  0.0 122.6 jit_solution(1750130739017493343)
XLA Ops:
  0.0 121.9 %shard_map.37 = bf16[128,256]{1,0:T(8,128)(2,1)S(1)} custom-call(bf16[32,1200,128]{2,1,0:T(8,128)(2,1)} %bitcast.7, bf16[1200,1200]{1,0:T(8,128)(2,1)} %bitcast.8, s32[1,128]{1,0:T(1,128)} %bitcast.9), custom_call_target="tpu_custom_call" | custom-call | tf_op jit(solution)/shard_map/pallas_call | solution.py:251
  121.9 0.6 copy.5

commit v7 on v6

--- a/solution.py
+++ b/solution.py
@@ -195,7 +195,7 @@
 
         def pass_on(slot, _):
             to = from_ref[slot]
-            for p, (src, dst) in enumerate(((screened, recv_s), (screened_t, recv_st))):
+            for p, (src, dst) in ((1, (screened_t, recv_st)), (0, (screened, recv_s))):
                 pltpu.make_async_remote_copy(
                     src.at[slot], dst.at[slot], send_sem.at[3 + p], recv_sem_s.at[p, lax.div(slot, FEW)],
                     device_id=(to,), device_id_type=MESH,
@@ -217,12 +217,13 @@
         places = [to_ref[g * FEW + i] for i in range(FEW)]
         mains = jnp.concatenate([own_main[q] for q in places], axis=0)
         tails = jnp.concatenate([own_tail[q] for q in places], axis=0)
-        for p, part in enumerate((recv_s, recv_st)):
-            view = part.at[slots]
-            pltpu.make_async_copy(view, view, recv_sem_s.at[p, g]).wait()
+        view = recv_st.at[slots]
+        pltpu.make_async_copy(view, view, recv_sem_s.at[1, g]).wait()
         ends = apart(recv_st[slots].reshape(FEW * HALF, 128))
-        every = lax.dot_general(mains, recv_s[slots].reshape(ROWS, MAIN), nt, preferred_element_type=F32)
-        every = every + lax.dot_general(tails, ends, nt, preferred_element_type=F32)
+        early = lax.dot_general(tails, ends, nt, preferred_element_type=F32)
+        view = recv_s.at[slots]
+        pltpu.make_async_copy(view, view, recv_sem_s.at[0, g]).wait()
+        every = early + lax.dot_general(mains, recv_s[slots].reshape(ROWS, MAIN), nt, preferred_element_type=F32)
         own = (every * same_q[...]).astype(BF16)
         wide = jnp.dot(own, spread[...], preferred_element_type=F32)
         wide = (wide * same_a[...]).astype(BF16)

time: 123 us -> 123 us (level)
  no operation moved by 1% of the time
where the time goes in v7:
time: 123 us; the launch traced here: 122 us
  Pallas kernels  122 us (99%)
    pallas_call x1, Pallas kernels, on_device(): pl.pallas_call(kernel, out_shape=jax.ShapeDtypeStruct((DEV, PAIRS * PAIRS...  122 us

profile of v7, /device:TPU:1, one launch (start us, length us, event | category | flops | bytes accessed | tf_op | source)
XLA Modules:
  0.0 122.4 jit_solution(12865498449828482910)
XLA Ops:
  0.0 121.8 %shard_map.37 = bf16[128,256]{1,0:T(8,128)(2,1)S(1)} custom-call(bf16[32,1200,128]{2,1,0:T(8,128)(2,1)} %bitcast.7, bf16[1200,1200]{1,0:T(8,128)(2,1)} %bitcast.8, s32[1,128]{1,0:T(1,128)} %bitcast.9), custom_call_target="tpu_custom_call" | custom-call | tf_op jit(solution)/shard_map/pallas_call | solution.py:252
  121.8 0.6 copy.5
